TPU v7x, 32 devices: a whole 2x2x4 slice. The times are simulated.
32 devices in a mesh: fsdp: 32 (over z, y, x, core).
Axes of the slice: x: 2, y: 2, z: 4, core: 2. Of those that a mesh axis runs over, the one named last changes fastest.
Arguments:
- block_input: bfloat16 [32, 196, 512], P('fsdp'), may hold values from -6 to 6
- out_cotangent: bfloat16 [32, 196, 512], P('fsdp'), may hold values from -6 to 6
- norm1_gain: bfloat16 [512], P('fsdp'), may hold values from 0.099609375 to 1.8984375
- norm1_bias: bfloat16 [512], P('fsdp'), may hold values from -3 to 3
- qkv_weight: bfloat16 [512, 1536], P('fsdp'), may hold values from -0.25 to 0.25
- qv_bias: bfloat16 [1024], P('fsdp'), may hold values from -3 to 3
- proj_weight: bfloat16 [512, 512], P('fsdp'), may hold values from -1 to 1
- proj_bias: bfloat16 [512], P('fsdp'), may hold values from -3 to 3
- norm2_gain: bfloat16 [512], P('fsdp'), may hold values from 0.099609375 to 1.8984375
- norm2_bias: bfloat16 [512], P('fsdp'), may hold values from -3 to 3
- fc1_weight: bfloat16 [512, 2048], P('fsdp'), may hold values from -0.25 to 0.25
- fc1_bias: bfloat16 [2048], P('fsdp'), may hold values from -3 to 3
- fc2_weight: bfloat16 [2048, 512], P(None, 'fsdp'), may hold values from -0.125 to 0.125
- fc2_bias: bfloat16 [512], P('fsdp'), may hold values from -3 to 3
- bias_table: bfloat16 [169, 16], replicated, may hold values from -4 to 296
- window_mask: int32 [4, 49, 49], replicated, may hold values from 0 to 1, as said below
- rel_index: int32 [49, 49], replicated, may hold values from 0 to 168
- partition: int32 [196], replicated, may hold values from 0 to 195, each once
Outputs:
- block_output: bfloat16 [32, 196, 512], P('fsdp')
- input_grad: float32 [32, 196, 512], P('fsdp')
- norm1_gain_grad: float32 [512], P('fsdp')
- norm1_bias_grad: float32 [512], P('fsdp')
- qkv_weight_grad: float32 [512, 1536], P('fsdp')
- qv_bias_grad: float32 [1024], P('fsdp')
- proj_weight_grad: float32 [512, 512], P('fsdp')
- proj_bias_grad: float32 [512], P('fsdp')
- norm2_gain_grad: float32 [512], P('fsdp')
- norm2_bias_grad: float32 [512], P('fsdp')
- fc1_weight_grad: float32 [512, 2048], P('fsdp')
- fc1_bias_grad: float32 [2048], P('fsdp')
- fc2_weight_grad: float32 [2048, 512], P(None, 'fsdp')
- fc2_bias_grad: float32 [512], P('fsdp')
- bias_table_grad: float32 [169, 16], replicated
Inputs may be any that keep to these rules, and one draw needn't show every extreme that they name: window_mask[w, i, j] is 1 exactly where positions i and j of window w carry the same region label; it is symmetric and 1 on the diagonal. `partition`: a permutation of 0 to 195.
All inputs are finite; a program needn't handle non-finite values.
Results may differ from a plain program's by a relative error of at most 0.011.
Values may be sent and summed in bfloat16 or wider, within the bound.
A program may use at most 128 MiB of HBM per device.

v0:
```python
import jax
import jax.numpy as jnp
from jax import lax
from jax.sharding import PartitionSpec as P

HEADS = 16
WINDOW = 49
WIN_IMG = 4
MICRO = 1
EPSILON = 1e-05
NEG_FILL = -1e30
ROOT_HALF = 0.7071067811865476
DENSITY = 0.3989422804014327


def normalize(values, gain_vec, shift_vec):
    center = values - jnp.mean(values, axis=-1, keepdims=True)
    inv_std = lax.rsqrt(jnp.mean(center * center, axis=-1, keepdims=True) + EPSILON)
    unit_rows = center * inv_std
    return (unit_rows * gain_vec + shift_vec, unit_rows, inv_std)


def norm_backward(grad_out, unit_rows, inv_std, gain_vec):
    scaled = grad_out * gain_vec
    grad_in = inv_std * (
        scaled
        - jnp.mean(scaled, axis=-1, keepdims=True)
        - unit_rows * jnp.mean(scaled * unit_rows, axis=-1, keepdims=True)
    )
    return (grad_in, jnp.sum(grad_out * unit_rows, axis=0), jnp.sum(grad_out, axis=0))


def gelu_parts(pre_act):
    normal_cdf = 0.5 * (1.0 + jax.scipy.special.erf(pre_act * ROOT_HALF))
    normal_pdf = jnp.exp(-0.5 * pre_act * pre_act) * DENSITY
    return (pre_act * normal_cdf, normal_cdf + pre_act * normal_pdf)


def to_windows(token_rows, partition):
    picked = jnp.take(token_rows, partition, axis=1)
    return picked.reshape(token_rows.shape[0], WIN_IMG, WINDOW, token_rows.shape[-1])


def from_windows(window_rows, inverse):
    flat_rows = window_rows.reshape(window_rows.shape[0], inverse.shape[0], window_rows.shape[-1])
    return jnp.take(flat_rows, inverse, axis=1)


def window_scores(queries, key_rows, lookups, score_scale):
    table_bias, allowed, partition, inverse = lookups
    raw = (
        jnp.einsum("bwihe,bwjhe->bwhij", queries, key_rows, preferred_element_type=jnp.float32)
        * score_scale
        + table_bias
    )
    return jnp.where(allowed, raw, NEG_FILL)


def fetch_pass_fwd(shards):
    return (
        lax.all_gather(shards[0], "fsdp", axis=0, tiled=True),
        lax.all_gather(shards[1], "fsdp", axis=0, tiled=True),
        lax.all_gather(shards[2], "fsdp", axis=0, tiled=True),
        lax.all_gather(shards[3], "fsdp", axis=0, tiled=True),
        lax.all_gather(shards[4], "fsdp", axis=0, tiled=True),
        lax.all_gather(shards[5], "fsdp", axis=0, tiled=True),
        lax.all_gather(shards[6], "fsdp", axis=0, tiled=True),
        lax.all_gather(shards[7], "fsdp", axis=0, tiled=True),
        lax.all_gather(shards[8], "fsdp", axis=0, tiled=True),
        lax.all_gather(shards[9], "fsdp", axis=0, tiled=True),
        lax.all_gather(shards[10], "fsdp", axis=1, tiled=True),
        lax.all_gather(shards[11], "fsdp", axis=0, tiled=True),
    )


def fetch_pass_bwd(shards):
    return (
        lax.all_gather(shards[0], "fsdp", axis=0, tiled=True),
        lax.all_gather(shards[1], "fsdp", axis=0, tiled=True),
        lax.all_gather(shards[2], "fsdp", axis=0, tiled=True),
        lax.all_gather(shards[3], "fsdp", axis=0, tiled=True),
        lax.all_gather(shards[4], "fsdp", axis=0, tiled=True),
        lax.all_gather(shards[5], "fsdp", axis=0, tiled=True),
        lax.all_gather(shards[6], "fsdp", axis=0, tiled=True),
        lax.all_gather(shards[7], "fsdp", axis=0, tiled=True),
        lax.all_gather(shards[8], "fsdp", axis=0, tiled=True),
        lax.all_gather(shards[9], "fsdp", axis=0, tiled=True),
        lax.all_gather(shards[10], "fsdp", axis=1, tiled=True),
        lax.all_gather(shards[11], "fsdp", axis=0, tiled=True),
    )


def scatter_whole(grads):
    return (
        lax.psum_scatter(grads[0], "fsdp", scatter_dimension=0, tiled=True),
        lax.psum_scatter(grads[1], "fsdp", scatter_dimension=0, tiled=True),
        lax.psum_scatter(grads[2], "fsdp", scatter_dimension=0, tiled=True),
        lax.psum_scatter(grads[3], "fsdp", scatter_dimension=0, tiled=True),
        lax.psum_scatter(grads[4], "fsdp", scatter_dimension=0, tiled=True),
        lax.psum_scatter(grads[5], "fsdp", scatter_dimension=0, tiled=True),
        lax.psum_scatter(grads[6], "fsdp", scatter_dimension=0, tiled=True),
        lax.psum_scatter(grads[7], "fsdp", scatter_dimension=0, tiled=True),
        lax.psum_scatter(grads[8], "fsdp", scatter_dimension=0, tiled=True),
        lax.psum_scatter(grads[9], "fsdp", scatter_dimension=0, tiled=True),
        lax.psum_scatter(grads[10], "fsdp", scatter_dimension=1, tiled=True),
        lax.psum_scatter(grads[11], "fsdp", scatter_dimension=0, tiled=True),
    )


def forward_pass(images, params, lookups):
    (
        gain_one,
        shift_one,
        qkv_weight,
        qv_bias,
        proj_weight,
        proj_bias,
        gain_two,
        shift_two,
        fc1_weight,
        fc1_bias,
        fc2_weight,
        fc2_bias,
    ) = params
    table_bias, allowed, partition, inverse = lookups
    image_count, tok_count, model_width = images.shape
    row_count = image_count * tok_count
    head_width = model_width // HEADS
    score_scale = head_width ** (-0.5)
    inputs_f = images.astype(jnp.float32).reshape(row_count, model_width)
    normed_one, unit_one, inv_one = normalize(
        inputs_f, gain_one.astype(jnp.float32), shift_one.astype(jnp.float32)
    )
    normed_one = normed_one.astype(jnp.bfloat16)
    qkv_shift = jnp.concatenate(
        [
            qv_bias[:model_width].astype(jnp.float32),
            jnp.zeros((model_width,), jnp.float32),
            qv_bias[model_width:].astype(jnp.float32),
        ]
    )
    qkv_rows = (
        jnp.dot(normed_one, qkv_weight, preferred_element_type=jnp.float32) + qkv_shift
    ).astype(jnp.bfloat16)
    qkv_win = to_windows(
        qkv_rows.reshape(image_count, tok_count, 3 * model_width), partition
    ).reshape(image_count, WIN_IMG, WINDOW, 3, HEADS, head_width)
    scores = window_scores(qkv_win[:, :, :, 0], qkv_win[:, :, :, 1], lookups, score_scale)
    row_top = jnp.max(scores, axis=-1, keepdims=True)
    log_total = row_top + jnp.log(jnp.sum(jnp.exp(scores - row_top), axis=-1, keepdims=True))
    soft_probs = jnp.exp(scores - log_total).astype(jnp.bfloat16)
    mixed = jnp.einsum(
        "bwhij,bwjhe->bwihe", soft_probs, qkv_win[:, :, :, 2], preferred_element_type=jnp.float32
    )
    attended = (
        from_windows(mixed.reshape(image_count, WIN_IMG, WINDOW, model_width), inverse)
        .astype(jnp.bfloat16)
        .reshape(row_count, model_width)
    )
    resid = (
        inputs_f
        + jnp.dot(attended, proj_weight, preferred_element_type=jnp.float32)
        + proj_bias.astype(jnp.float32)
    )
    normed_two, unit_two, inv_two = normalize(
        resid, gain_two.astype(jnp.float32), shift_two.astype(jnp.float32)
    )
    normed_two = normed_two.astype(jnp.bfloat16)
    pre_act = jnp.dot(normed_two, fc1_weight, preferred_element_type=jnp.float32) + fc1_bias.astype(
        jnp.float32
    )
    activ, gelu_slope = gelu_parts(pre_act)
    activ = activ.astype(jnp.bfloat16)
    output = (
        resid
        + jnp.dot(activ, fc2_weight, preferred_element_type=jnp.float32)
        + fc2_bias.astype(jnp.float32)
    ).astype(jnp.bfloat16)
    saved = (
        unit_one,
        inv_one,
        normed_one,
        qkv_win,
        log_total,
        attended,
        unit_two,
        inv_two,
        normed_two,
        gelu_slope,
        activ,
    )
    return (output.reshape(image_count, tok_count, model_width), saved)


def backward_pass(cotangent, saved, params, lookups):
    (
        gain_one,
        shift_one,
        qkv_weight,
        qv_bias,
        proj_weight,
        proj_bias,
        gain_two,
        shift_two,
        fc1_weight,
        fc1_bias,
        fc2_weight,
        fc2_bias,
    ) = params
    (
        unit_one,
        inv_one,
        normed_one,
        qkv_win,
        log_total,
        attended,
        unit_two,
        inv_two,
        normed_two,
        gelu_slope,
        activ,
    ) = saved
    table_bias, allowed, partition, inverse = lookups
    image_count, tok_count, model_width = cotangent.shape
    row_count = image_count * tok_count
    head_width = model_width // HEADS
    score_scale = head_width ** (-0.5)
    cot_rows = cotangent.reshape(row_count, model_width)
    cot_f = cot_rows.astype(jnp.float32)
    fc2_grad = jnp.dot(activ.T, cot_rows, preferred_element_type=jnp.float32)
    fc2_bias_grad = jnp.sum(cot_f, axis=0)
    grad_pre = jnp.dot(cot_rows, fc2_weight.T, preferred_element_type=jnp.float32) * gelu_slope
    grad_pre_b = grad_pre.astype(jnp.bfloat16)
    fc1_grad = jnp.dot(normed_two.T, grad_pre_b, preferred_element_type=jnp.float32)
    fc1_bias_grad = jnp.sum(grad_pre, axis=0)
    grad_normed = jnp.dot(grad_pre_b, fc1_weight.T, preferred_element_type=jnp.float32)
    grad_mid, gain_two_grad, shift_two_grad = norm_backward(
        grad_normed, unit_two, inv_two, gain_two.astype(jnp.float32)
    )
    grad_resid = cot_f + grad_mid
    grad_resid_b = grad_resid.astype(jnp.bfloat16)
    proj_grad = jnp.dot(attended.T, grad_resid_b, preferred_element_type=jnp.float32)
    proj_bias_grad = jnp.sum(grad_resid, axis=0)
    grad_att = jnp.dot(grad_resid_b, proj_weight.T, preferred_element_type=jnp.float32).astype(
        jnp.bfloat16
    )
    grad_mixed = to_windows(
        grad_att.reshape(image_count, tok_count, model_width), partition
    ).reshape(image_count, WIN_IMG, WINDOW, HEADS, head_width)
    queries = qkv_win[:, :, :, 0]
    key_rows = qkv_win[:, :, :, 1]
    value_rows = qkv_win[:, :, :, 2]
    scores = window_scores(queries, key_rows, lookups, score_scale)
    soft_full = jnp.exp(scores - log_total)
    soft_probs = soft_full.astype(jnp.bfloat16)
    value_grad = jnp.einsum(
        "bwhij,bwihe->bwjhe", soft_probs, grad_mixed, preferred_element_type=jnp.float32
    )
    prob_grad = jnp.einsum(
        "bwihe,bwjhe->bwhij", grad_mixed, value_rows, preferred_element_type=jnp.float32
    )
    score_grad = soft_full * (prob_grad - jnp.sum(soft_full * prob_grad, axis=-1, keepdims=True))
    pair_grad = jnp.sum(score_grad, axis=(0, 1))
    score_grad_b = score_grad.astype(jnp.bfloat16)
    query_grad = (
        jnp.einsum("bwhij,bwjhe->bwihe", score_grad_b, key_rows, preferred_element_type=jnp.float32)
        * score_scale
    )
    key_grad = (
        jnp.einsum("bwhij,bwihe->bwjhe", score_grad_b, queries, preferred_element_type=jnp.float32)
        * score_scale
    )
    stacked = jnp.stack([query_grad, key_grad, value_grad], axis=3).reshape(
        image_count, WIN_IMG, WINDOW, 3 * model_width
    )
    qkv_grad = from_windows(stacked, inverse).reshape(row_count, 3 * model_width)
    qkv_grad_b = qkv_grad.astype(jnp.bfloat16)
    qkv_grad_w = jnp.dot(normed_one.T, qkv_grad_b, preferred_element_type=jnp.float32)
    column_sums = jnp.sum(qkv_grad, axis=0)
    qv_grad = jnp.concatenate([column_sums[:model_width], column_sums[2 * model_width :]])
    grad_first = jnp.dot(qkv_grad_b, qkv_weight.T, preferred_element_type=jnp.float32)
    grad_low, gain_one_grad, shift_one_grad = norm_backward(
        grad_first, unit_one, inv_one, gain_one.astype(jnp.float32)
    )
    input_grad = (grad_resid + grad_low).reshape(image_count, tok_count, model_width)
    grads = (
        gain_one_grad,
        shift_one_grad,
        qkv_grad_w,
        qv_grad,
        proj_grad,
        proj_bias_grad,
        gain_two_grad,
        shift_two_grad,
        fc1_grad,
        fc1_bias_grad,
        fc2_grad,
        fc2_bias_grad,
    )
    return (input_grad, grads, pair_grad)


def per_device(
    block_input,
    out_cotangent,
    norm1_gain,
    norm1_bias,
    qkv_weight,
    qv_bias,
    proj_weight,
    proj_bias,
    norm2_gain,
    norm2_bias,
    fc1_weight,
    fc1_bias,
    fc2_weight,
    fc2_bias,
    bias_table,
    window_mask,
    rel_index,
    partition,
):
    shards = (
        norm1_gain,
        norm1_bias,
        qkv_weight,
        qv_bias,
        proj_weight,
        proj_bias,
        norm2_gain,
        norm2_bias,
        fc1_weight,
        fc1_bias,
        fc2_weight,
        fc2_bias,
    )
    pair_count = WINDOW * WINDOW
    table_rows = bias_table.shape[0]
    one_hot = (
        rel_index.reshape(pair_count, 1) == jnp.arange(table_rows, dtype=jnp.int32)[None, :]
    ).astype(jnp.float32)
    table_bias = jnp.transpose(
        jnp.dot(one_hot, bias_table.astype(jnp.float32), precision=lax.Precision.HIGHEST).reshape(
            WINDOW, WINDOW, HEADS
        ),
        (2, 0, 1),
    )
    allowed = (window_mask == 1)[None, :, None, :, :]
    tok_count = partition.shape[0]
    inverse = (
        jnp.zeros((tok_count,), jnp.int32).at[partition].set(jnp.arange(tok_count, dtype=jnp.int32))
    )
    lookups = (table_bias, allowed, partition, inverse)
    held_params = fetch_pass_fwd(shards)
    micro_index = 0
    output, saved = forward_pass(block_input, held_params, lookups)
    kept = [saved]
    held_params = fetch_pass_bwd(shards)
    input_grads = [None] * MICRO
    pair_total = jnp.zeros((HEADS, WINDOW, WINDOW), jnp.float32)
    grad_totals = None
    for micro_index in reversed(range(MICRO)):
        input_grad, grads, pair_grad = backward_pass(
            out_cotangent, kept[micro_index], held_params, lookups
        )
        input_grads[micro_index] = input_grad
        pair_total = pair_grad
        grad_totals = grads
    grad_totals = scatter_whole(grad_totals)
    table_local = jnp.dot(
        one_hot.T,
        jnp.transpose(pair_total, (1, 2, 0)).reshape(pair_count, HEADS),
        precision=lax.Precision.HIGHEST,
    )
    table_grad = lax.psum(table_local, "fsdp")
    input_grad_all = input_grads[0]
    return (
        output,
        input_grad_all,
        grad_totals[0],
        grad_totals[1],
        grad_totals[2],
        grad_totals[3],
        grad_totals[4],
        grad_totals[5],
        grad_totals[6],
        grad_totals[7],
        grad_totals[8],
        grad_totals[9],
        grad_totals[10],
        grad_totals[11],
        table_grad,
    )


def solution(mesh):
    placed = (
        P("fsdp", None, None),
        P("fsdp", None, None),
        P("fsdp"),
        P("fsdp"),
        P("fsdp", None),
        P("fsdp"),
        P("fsdp", None),
        P("fsdp"),
        P("fsdp"),
        P("fsdp"),
        P("fsdp", None),
        P("fsdp"),
        P(None, "fsdp"),
        P("fsdp"),
        P(),
        P(),
        P(),
        P(),
    )
    return jax.shard_map(
        per_device,
        mesh=mesh,
        in_specs=placed,
        out_specs=(
            P("fsdp", None, None),
            P("fsdp", None, None),
            P("fsdp"),
            P("fsdp"),
            P("fsdp", None),
            P("fsdp"),
            P("fsdp", None),
            P("fsdp"),
            P("fsdp"),
            P("fsdp"),
            P("fsdp", None),
            P("fsdp"),
            P(None, "fsdp"),
            P("fsdp"),
            P(),
        ),
        check_vma=False,
    )
```

profile of v0, /device:TPU:0, one launch (start us, length us, event | category | flops | bytes accessed | tf_op | source)
XLA Modules:
  0.0 725.9 jit_solution(5990578621208779468)
XLA Ops:
  18.9 42.4 %all-reduce.17 = (bf16[512]{0:T(512)(128)(2,1)S(1)}, bf16[1024]{0:T(1024)(128)(2,1)S(1)}, bf16[512]{0:T(512)(128)(2,1)S(1)}, bf16[512]{0:T(512)(128)(2,1)S(1)}, ...) all-reduce(bf16[512]{0:T(512)(128)(2,1)S(1)} %dynamic-update-slice., ...), channel_id=1, replica_groups=mesh['fsdp'=32] {'fsdp'}, use_global_device_ids=true, to_apply=%add.3 | all-reduce | flops 6144 | bytes 24576
  66.3 45.4 %all_gather.46 = bf16[512,512]{1,0:T(8,128)(2,1)} all-gather(bf16[16,512]{1,0:T(8,128)(2,1)S(1)} %copy-done.15), channel_id=1, replica_groups=mesh['fsdp'=32] {'fsdp'}, dimensions={0}, use_global_device_ids=true | all-gather | bytes 540672 | tf_op jit(solution)/shard_map/all_gather | solution.py:65
  111.7 2.0 fusion
  116.4 3.0 copy.58
  124.3 1.9 reshape.401
  128.0 3.6 multiply_convert_fusion
  131.6 53.5 %all-gather.8.cloned.1.call-done = bf16[2048,512]{0,1:T(8,128)(2,1)} async-done(((bf16[2048,16]{0,1:T(8,128)(2,1)}), bf16[2048,512]{0,1:T(8,128)(2,1)}) %all-gather.8.cloned.1.call-update) | async-done | bytes 2097168 | tf_op jit(solution)/shard_map/all_gather | solution.py:71
  185.0 3.9 fusion.82
  198.7 2.1 gather.31
  202.0 1.8 multiply_reduce_fusion
  206.9 2.0 pad_maximum_fusion
  208.9 5.8 copy.81
  214.7 4.0 reshape.402
  218.7 2.1 gather_fusion.3
  220.8 3.8 fusion.19
  225.8 2.8 fusion.50
  229.5 2.7 fusion.59
  235.5 2.3 fusion.44
  240.4 39.1 %all-reduce.16 = (f32[512]{0:T(512)S(1)}, f32[512]{0:T(512)S(1)}, f32[1024]{0:T(1024)S(1)}, f32[512]{0:T(512)S(1)}, f32[512]{0:T(512)S(1)}, /*index=5*/f32[512]{...) all-reduce(f32[512]{0:T(512)S(1)} %get-tuple-element.62, ...), channel_id=2, replica_groups=mesh['fsdp'=32] {'fsdp'}, use_global_device_ids=true, to_apply=%region_13.14.clone | all-reduce | flops 8848 | bytes 70784
  284.2 3.2 fusion.16
  287.4 41.9 %reduce-scatter.7.cloned.1.call-done = f32[16,512]{1,0:T(8,128)} async-done(((f32[512,512]{1,0:T(8,128)}), f32[16,512]{1,0:T(8,128)}) %reduce-scatter.7.cloned.1.call-update) | async-done | bytes 32784 | tf_op jit(solution)/shard_map/reduce_scatter | solution.py:99
  329.3 104.0 %reduce-scatter.5.cloned.1.call-done = f32[16,1536]{1,0:T(8,128)} async-done(((f32[512,1536]{1,0:T(8,128)}), f32[16,1536]{1,0:T(8,128)}) %reduce-scatter.5.cloned.1.call-update) | async-done | bytes 98320 | tf_op jit(solution)/shard_map/reduce_scatter | solution.py:97
  433.3 144.1 %reduce-scatter.9.cloned.1.call-done = f32[16,2048]{1,0:T(8,128)} async-done(((f32[512,2048]{1,0:T(8,128)}), f32[16,2048]{1,0:T(8,128)}) %reduce-scatter.9.cloned.1.call-update) | async-done | bytes 131088 | tf_op jit(solution)/shard_map/reduce_scatter | solution.py:103
  577.4 141.6 %reduce-scatter.11.cloned.1.call-done = f32[2048,16]{0,1:T(8,128)} async-done(((f32[2048,512]{0,1:T(8,128)}), f32[2048,16]{0,1:T(8,128)}) %reduce-scatter.11.cloned.1.call-update) | async-done | bytes 131088 | tf_op jit(solution)/shard_map/reduce_scatter | solution.py:105
  (170 shorter events, 52.0 us)
Async XLA Ops:
  7.2 56.0 %copy-start = (bf16[169,16]{0,1:T(8,128)(2,1)S(1)}, bf16[169,16]{0,1:T(8,128)(2,1)}, u32[]{:S(2)}) copy-start(bf16[169,16]{0,1:T(8,128)(2,1)} %param.32) | copy-start | bytes 16228
  7.2 58.7 %copy-start.6 = (bf16[1,196,512]{2,1,0:T(8,128)(2,1)S(1)}, bf16[1,196,512]{2,1,0:T(8,128)(2,1)}, u32[]{:S(2)}) copy-start(bf16[1,196,512]{2,1,0:T(8,128)(2,1)} %param.18) | copy-start | bytes 602116
  7.2 59.1 %copy-start.15 = (bf16[16,512]{1,0:T(8,128)(2,1)S(1)}, bf16[16,512]{1,0:T(8,128)(2,1)}, u32[]{:S(2)}) copy-start(bf16[16,512]{1,0:T(8,128)(2,1)} %param.24) | copy-start | bytes 49156
  7.2 104.5 %all-gather.4.cloned.1.call-start = ((), (), s32[]{:S(2)}) async-start(), calls=%async_computation.4 | async-start | bytes 1622016 | tf_op jit(solution)/shard_map/all_gather | solution.py:63
  7.9 120.0 %all-gather.6.cloned.1.call-start = ((), (), s32[]{:S(2)}) async-start(), calls=%async_computation.5 | async-start | bytes 2162688 | tf_op jit(solution)/shard_map/all_gather | solution.py:69
  8.7 176.3 %all-gather.8.cloned.1.call-start = ((), (), s32[]{:S(2)}) async-start(), calls=%async_computation.6 | async-start | bytes 2162688 | tf_op jit(solution)/shard_map/all_gather | solution.py:71
  9.4 319.9 %reduce-scatter.7.cloned.1.call-start = ((), (), s32[]{:S(2)}) async-start(), calls=%async_computation.8 | async-start | bytes 1081344 | tf_op jit(solution)/shard_map/reduce_scatter | solution.py:99
  63.8 55.6 %copy-start.30 = (pred[4,49]{1,0:T(4,128)(4,1)}, pred[4,49]{1,0:T(4,128)(4,1)S(1)}, u32[]{:S(2)}) copy-start(pred[4,49]{1,0:T(4,128)(4,1)S(1)} %broadcast_in_dim.97) | copy-start | bytes 592
  64.4 49.2 %copy-start.20 = (f32[512]{0:T(512)}, f32[512]{0:T(512)S(1)}, u32[]{:S(2)}) copy-start(f32[512]{0:T(512)S(1)} %convert_element_type.103) | copy-start | bytes 6148
  66.2 61.1 %copy-start.22 = (pred[196]{0:T(512)(128)(4,1)}, pred[196]{0:T(512)(128)(4,1)S(1)}, u32[]{:S(2)}) copy-start(pred[196]{0:T(512)(128)(4,1)S(1)} %compare_and_fusion.1) | copy-start | bytes 592
  66.3 48.5 %copy-start.18 = (f32[196]{0:T(256)}, f32[196]{0:T(256)S(1)}, u32[]{:S(2)}) copy-start(f32[196]{0:T(256)S(1)} %add_rsqrt_fusion.1) | copy-start | bytes 2356
  124.3 3.0 copy-start.7
  124.3 3.0 copy-start.26
  185.0 3.9 copy-start.8
  188.9 3.1 copy-start.23
  193.5 239.8 %reduce-scatter.5.cloned.1.call-start = ((), (), s32[]{:S(2)}) async-start(), calls=%async_computation.7 | async-start | bytes 3244032 | tf_op jit(solution)/shard_map/reduce_scatter | solution.py:97
  195.2 5.5 copy-start.31
  224.6 352.8 %reduce-scatter.9.cloned.1.call-start = ((), (), s32[]{:S(2)}) async-start(), calls=%async_computation.9 | async-start | bytes 4325376 | tf_op jit(solution)/shard_map/reduce_scatter | solution.py:103
  228.6 490.5 %reduce-scatter.11.cloned.1.call-start = ((), (), s32[]{:S(2)}) async-start(), calls=%async_computation.10 | async-start | bytes 4325376 | tf_op jit(solution)/shard_map/reduce_scatter | solution.py:105
  232.2 3.2 copy-start.1
  235.5 2.3 copy-start.5
  238.0 2.3 copy-start.24
  238.1 2.3 copy-start.25
  238.1 2.3 copy-start.27
  (16 other events, 24.6 us)
Sparse Core Ops, SparseCore 0:
  10.9 57.9 all-gather.3
  71.7 55.2 all-gather.5
  130.0 55.0 all-gather.7
  193.6 135.6 reduce-scatter.6
  335.2 98.0 reduce-scatter.4
  436.0 141.3 reduce-scatter.8
  580.3 138.7 reduce-scatter.10
where the time goes:
time: 727 us; the launch traced here: 726 us
  waiting for transfers between devices  487 us (67%)
  blocking collectives  127 us (17%)
  local copies, waits for them, and re-layouts  49.8 us (7%)
  matrix products  35.1 us (5%)
  between operations  14.7 us (2%)
  other arithmetic  11.5 us (2%)
    reduce_scatter x1, waiting for transfers between devices, scatter_whole(): lax.psum_scatter(grads[8], 'fsdp', scatter_dimension=0, tiled=True)  144 us
    reduce_scatter x1, waiting for transfers between devices, scatter_whole(): lax.psum_scatter(grads[10], 'fsdp', scatter_dimension=1, tiled=True)  142 us
    reduce_scatter x1, waiting for transfers between devices, scatter_whole(): lax.psum_scatter(grads[2], 'fsdp', scatter_dimension=0, tiled=True)  104 us
    unnamed x2, blocking collectives  81.6 us
    all_gather x1, waiting for transfers between devices, fetch_pass_fwd(): lax.all_gather(shards[10], 'fsdp', axis=1, tiled=True)  53.5 us
    all_gather x1, blocking collectives, fetch_pass_fwd(): lax.all_gather(shards[4], 'fsdp', axis=0, tiled=True)  45.4 us
    reduce_scatter x1, waiting for transfers between devices, scatter_whole(): lax.psum_scatter(grads[4], 'fsdp', scatter_dimension=0, tiled=True)  41.9 us
    unnamed x91, local copies, waits for them, and re-layouts  16.4 us
  transfers between devices with their start and end apart: 7, of which 5 were waited for; matrix products, arithmetic and copies ran while one was open for 12% of the time, Pallas kernels for 0%

commit v1 on v0

--- a/solution.py
+++ b/solution.py
@@ -11,6 +11,18 @@
 NEG_FILL = -1e30
 ROOT_HALF = 0.7071067811865476
 DENSITY = 0.3989422804014327
+
+
+def gather_by_bits(shard, axis, dim):
+    ways, here = (lax.axis_size(axis), lax.axis_index(axis))
+    grown, reach = (shard, 1)
+    while reach < ways:
+        theirs = lax.ppermute(grown, axis, [(d, d ^ reach) for d in range(ways)])
+        mine_first = jnp.concatenate([grown, theirs], axis=dim)
+        theirs_first = jnp.concatenate([theirs, grown], axis=dim)
+        grown = jnp.where(here & reach == 0, mine_first, theirs_first)
+        reach = 2 * reach
+    return grown
 
 
 def normalize(values, gain_vec, shift_vec):
@@ -68,7 +80,7 @@
         lax.all_gather(shards[7], "fsdp", axis=0, tiled=True),
         lax.all_gather(shards[8], "fsdp", axis=0, tiled=True),
         lax.all_gather(shards[9], "fsdp", axis=0, tiled=True),
-        lax.all_gather(shards[10], "fsdp", axis=1, tiled=True),
+        gather_by_bits(shards[10], "fsdp", 1),
         lax.all_gather(shards[11], "fsdp", axis=0, tiled=True),
     )
 

time: 727 us -> 727 us (level)
  waiting for transfers between devices: 487 us -> 466 us
  blocking collectives: 127 us -> 147 us
    reduce_scatter x1, waiting for transfers between devices: 41.9 us -> 0.01 us  [scatter_whole(): lax.psum_scatter(grads[4], 'fsdp', scatter_dimension=0, tiled=True)]
    ppermute x0 -> x5, waiting for transfers between devices: none -> 23.8 us  [gather_by_bits(): theirs = lax.ppermute(grown, axis, [(d, d ^ reach) for d in range(ways)])]
    unnamed x2, blocking collectives: 81.6 us -> 105 us
    unnamed x91 -> x71, local copies, waits for them, and re-layouts: 16.4 us -> 15.5 us
  transfers between devices with their start and end apart: 7 -> 12, of which waited for: 5 -> 9; matrix products, arithmetic and copies ran while one was open for 12% -> 11% of each run, Pallas kernels for 0% -> 0%
where the time goes in v1:
time: 727 us
  waiting for transfers between devices  466 us (64%)
  blocking collectives  147 us (20%)
  local copies, waits for them, and re-layouts  46.6 us (6%)
  matrix products  31.5 us (4%)
  between operations  14.6 us (2%)
  other arithmetic  13.8 us (2%)
    reduce_scatter x1, waiting for transfers between devices, scatter_whole(): lax.psum_scatter(grads[8], 'fsdp', scatter_dimension=0, tiled=True)  145 us
    reduce_scatter x1, waiting for transfers between devices, scatter_whole(): lax.psum_scatter(grads[10], 'fsdp', scatter_dimension=1, tiled=True)  141 us
    unnamed x2, blocking collectives  105 us
    reduce_scatter x1, waiting for transfers between devices, scatter_whole(): lax.psum_scatter(grads[2], 'fsdp', scatter_dimension=0, tiled=True)  99.7 us
    all_gather x1, waiting for transfers between devices, fetch_pass_bwd(): lax.all_gather(shards[10], 'fsdp', axis=1, tiled=True)  54.1 us
    all_gather x1, blocking collectives, fetch_pass_fwd(): lax.all_gather(shards[4], 'fsdp', axis=0, tiled=True)  42.1 us
    ppermute x5, waiting for transfers between devices, gather_by_bits(): theirs = lax.ppermute(grown, axis, [(d, d ^ reach) for d in range(ways)])  23.8 us
    unnamed x71, local copies, waits for them, and re-layouts  15.5 us
  transfers between devices with their start and end apart: 12, of which 9 were waited for; matrix products, arithmetic and copies ran while one was open for 11% of the time, Pallas kernels for 0%

profile of v1, /device:TPU:0, one launch (start us, length us, event | category | flops | bytes accessed | tf_op | source)
XLA Modules:
  0.0 726.5 jit_solution(3827827915900402050)
XLA Ops:
  17.6 42.5 %all-reduce.17 = (bf16[512]{0:T(512)(128)(2,1)S(1)}, bf16[1024]{0:T(1024)(128)(2,1)S(1)}, bf16[512]{0:T(512)(128)(2,1)S(1)}, bf16[512]{0:T(512)(128)(2,1)S(1)}, ...) all-reduce(bf16[512]{0:T(512)(128)(2,1)S(1)} %dynamic-update-slice., ...), channel_id=1, replica_groups=mesh['fsdp'=32] {'fsdp'}, use_global_device_ids=true, to_apply=%add.3 | all-reduce | flops 6144 | bytes 24576
  65.7 42.1 %all_gather.45 = bf16[512,512]{1,0:T(8,128)(2,1)S(1)} all-gather(bf16[16,512]{1,0:T(8,128)(2,1)S(1)} %copy-done.19), channel_id=1, replica_groups=mesh['fsdp'=32] {'fsdp'}, dimensions={0}, use_global_device_ids=true | all-gather | bytes 540672 | tf_op jit(solution)/shard_map/all_gather | solution.py:77
  107.8 2.0 fusion
  109.8 1.9 gather_fusion
  111.7 2.9 reshape.400
  114.7 3.1 copy.58
  127.0 3.9 multiply_convert_fusion
  130.8 54.1 %all-gather.8.cloned.1.call-done = bf16[2048,512]{0,1:T(8,128)(2,1)} async-done(((bf16[2048,16]{0,1:T(8,128)(2,1)}), bf16[2048,512]{0,1:T(8,128)(2,1)}) %all-gather.8.cloned.1.call-update) | async-done | bytes 2097168 | tf_op jit(solution)/shard_map/all_gather | solution.py:100
  184.9 3.8 fusion.91
  196.7 2.1 gather.31
  204.3 4.0 copy.81
  208.2 4.0 reshape.402
  213.3 2.5 fusion.27
  217.1 2.8 fusion.58
  221.1 2.7 fusion.67
  227.4 4.2 collective-permute-done.1
  233.5 6.3 collective-permute-done.2
  242.0 12.3 %collective-permute-done.3 = bf16[2048,128]{0,1:T(8,128)(2,1)} collective-permute-done((bf16[2048,128]{0,1:T(8,128)(2,1)}, bf16[2048,128]{0,1:T(8,128)(2,1)}, u32[]{:S(2)}, u32[]{:S(2)}) %collective-permute-start.3) | collective-permute-done | bytes 524320 | tf_op jit(solution)/shard_map/ppermute | solution.py:20
  254.3 3.0 maximum_select_fusion.10
  262.8 62.7 %all-reduce.16 = (f32[512]{0:T(512)S(1)}, f32[512]{0:T(512)S(1)}, f32[1024]{0:T(1024)S(1)}, f32[512]{0:T(512)S(1)}, f32[512]{0:T(512)S(1)}, /*index=5*/f32[512]{...) all-reduce(f32[512]{0:T(512)} %get-tuple-element.62, ...), channel_id=2, replica_groups=mesh['fsdp'=32] {'fsdp'}, use_global_device_ids=true, to_apply=%region_13.14.clone | all-reduce | flops 8848 | bytes 70784
  330.1 3.8 fusion.24
  334.0 99.7 %reduce-scatter.5.cloned.1.call-done = f32[16,1536]{1,0:T(8,128)} async-done(((f32[512,1536]{1,0:T(8,128)}), f32[16,1536]{1,0:T(8,128)}) %reduce-scatter.5.cloned.1.call-update) | async-done | bytes 98320 | tf_op jit(solution)/shard_map/reduce_scatter | solution.py:109
  433.6 144.6 %reduce-scatter.9.cloned.1.call-done = f32[16,2048]{1,0:T(8,128)} async-done(((f32[512,2048]{1,0:T(8,128)}), f32[16,2048]{1,0:T(8,128)}) %reduce-scatter.9.cloned.1.call-update) | async-done | bytes 131088 | tf_op jit(solution)/shard_map/reduce_scatter | solution.py:115
  578.2 141.5 %reduce-scatter.11.cloned.1.call-done = f32[2048,16]{0,1:T(8,128)} async-done(((f32[2048,512]{0,1:T(8,128)}), f32[2048,16]{0,1:T(8,128)}) %reduce-scatter.11.cloned.1.call-update) | async-done | bytes 131088 | tf_op jit(solution)/shard_map/reduce_scatter | solution.py:117
  (164 shorter events, 59.6 us)
Async XLA Ops:
  7.2 56.0 %copy-start = (bf16[169,16]{0,1:T(8,128)(2,1)S(1)}, bf16[169,16]{0,1:T(8,128)(2,1)}, u32[]{:S(2)}) copy-start(bf16[169,16]{0,1:T(8,128)(2,1)} %param.32) | copy-start | bytes 16228
  7.2 58.1 %copy-start.8 = (bf16[1,196,512]{2,1,0:T(8,128)(2,1)S(1)}, bf16[1,196,512]{2,1,0:T(8,128)(2,1)}, u32[]{:S(2)}) copy-start(bf16[1,196,512]{2,1,0:T(8,128)(2,1)} %param.18) | copy-start | bytes 602116
  7.2 58.5 %copy-start.19 = (bf16[16,512]{1,0:T(8,128)(2,1)S(1)}, bf16[16,512]{1,0:T(8,128)(2,1)}, u32[]{:S(2)}) copy-start(bf16[16,512]{1,0:T(8,128)(2,1)} %param.24) | copy-start | bytes 49156
  7.2 100.6 %all-gather.4.cloned.1.call-start = ((), (), s32[]{:S(2)}) async-start(), calls=%async_computation.4 | async-start | bytes 1622016 | tf_op jit(solution)/shard_map/all_gather | solution.py:75
  7.9 119.0 %all-gather.6.cloned.1.call-start = ((), (), s32[]{:S(2)}) async-start(), calls=%async_computation.5 | async-start | bytes 2162688 | tf_op jit(solution)/shard_map/all_gather | solution.py:81
  8.7 176.2 %all-gather.8.cloned.1.call-start = ((), (), s32[]{:S(2)}) async-start(), calls=%async_computation.6 | async-start | bytes 2162688 | tf_op jit(solution)/shard_map/all_gather | solution.py:100
  9.4 324.5 %reduce-scatter.7.cloned.1.call-start = ((), (), s32[]{:S(2)}) async-start(), calls=%async_computation.8 | async-start | bytes 1081344 | tf_op jit(solution)/shard_map/reduce_scatter | solution.py:111
  61.0 2.8 copy-start.20
  126.0 64.2 %copy-start.1 = (f32[196,512]{1,0:T(8,128)}, f32[196,512]{1,0:T(8,128)S(1)}, u32[]{:S(2)}) copy-start(f32[196,512]{1,0:T(8,128)S(1)} %get-tuple-element.97) | copy-start | bytes 1204228
  126.2 58.7 %copy-start.12 = (bf16[1,196,512]{2,1,0:T(8,128)(2,1)S(1)}, bf16[1,196,512]{2,1,0:T(8,128)(2,1)}, u32[]{:S(2)}) copy-start(bf16[1,196,512]{2,1,0:T(8,128)(2,1)} %param.19) | copy-start | bytes 602116
  184.9 3.8 copy-start.10
  191.0 2.0 copy-start.5
  192.5 241.2 %reduce-scatter.5.cloned.1.call-start = ((), (), s32[]{:S(2)}) async-start(), calls=%async_computation.7 | async-start | bytes 3244032 | tf_op jit(solution)/shard_map/reduce_scatter | solution.py:109
  194.8 5.2 copy-start.4
  215.8 362.4 %reduce-scatter.9.cloned.1.call-start = ((), (), s32[]{:S(2)}) async-start(), calls=%async_computation.9 | async-start | bytes 4325376 | tf_op jit(solution)/shard_map/reduce_scatter | solution.py:115
  219.9 499.8 %reduce-scatter.11.cloned.1.call-start = ((), (), s32[]{:S(2)}) async-start(), calls=%async_computation.10 | async-start | bytes 4325376 | tf_op jit(solution)/shard_map/reduce_scatter | solution.py:117
  224.7 1.3 collective-permute-start
  225.9 5.7 collective-permute-start.1
  231.7 8.1 %collective-permute-start.2 = (bf16[2048,64]{0,1:T(8,128)(2,1)S(1)}, bf16[2048,64]{0,1:T(8,128)(2,1)S(1)}, u32[]{:S(2)}, u32[]{:S(2)}) collective-permute-start(bf16[2048,64]{0,1:T(8,128)(2,1)S(1)} %maximum_select_fusion.12), channel_id=1, source_target_pairs={{0,4},{1,5},{2,6},{3,7},{4,0},{5,1},{6,2},{7,3},{8,12},{9,13},{10,... | collective-permute-start | bytes 786440 | tf_op jit(solution)/shard_map/ppermute | solution.py:20
  240.7 13.5 %collective-permute-start.3 = (bf16[2048,128]{0,1:T(8,128)(2,1)}, bf16[2048,128]{0,1:T(8,128)(2,1)}, u32[]{:S(2)}, u32[]{:S(2)}) collective-permute-start(bf16[2048,128]{0,1:T(8,128)(2,1)} %maximum_select_fusion.11), channel_id=1, source_target_pairs={{0,8},{1,9},{2,10},{3,11},{4,12},{5,13},{6,14},{7,15},{8,0},{9,1},... | collective-permute-start | bytes 1572872 | tf_op jit(solution)/shard_map/ppermute | solution.py:20
  242.0 16.5 %copy-start.22 = (bf16[512,1536]{1,0:T(8,128)(2,1)S(1)}, bf16[512,1536]{1,0:T(8,128)(2,1)}, u32[]{:S(2)}) copy-start(bf16[512,1536]{1,0:T(8,128)(2,1)} %all-gather.4.cloned.1.call-done) | copy-start | bytes 4718596
  257.3 2.6 copy-start.6
  257.3 72.9 %collective-permute-start.4 = (bf16[2048,256]{0,1:T(8,128)(2,1)}, bf16[2048,256]{0,1:T(8,128)(2,1)}, u32[]{:S(2)}, u32[]{:S(2)}) collective-permute-start(bf16[2048,256]{0,1:T(8,128)(2,1)} %maximum_select_fusion.10), channel_id=1, source_target_pairs={{0,16},{1,17},{2,18},{3,19},{4,20},{5,21},{6,22},{7,23},{8,24},{9,... | collective-permute-start | bytes 3145736 | tf_op jit(solution)/shard_map/ppermute | solution.py:20
  260.0 1.8 copy-start.21
  (11 other events, 13.7 us)
Sparse Core Ops, SparseCore 0:
  10.9 57.9 all-gather.3
  71.8 55.1 all-gather.5
  129.8 55.0 all-gather.7
  192.6 136.9 reduce-scatter.6
  335.5 98.1 reduce-scatter.4
  436.4 141.8 reduce-scatter.8
  581.0 138.5 reduce-scatter.10
